TPU v7x, 32 devices: a whole 2x2x4 slice. The times are simulated.
32 devices in a mesh: seq: 4 (over x, core), span: 8 (over z, y).
Axes of the slice: x: 2, y: 2, z: 4, core: 2. Of those that a mesh axis runs over, the one named last changes fastest.
Arguments:
- llm_input: bfloat16 [512, 5120], P(('seq', 'span')), may hold values from -6 to 6
- hidden_grad: bfloat16 [512, 32768], P(None, ('seq', 'span')), may hold values from -1.5 to 1.5
- gate_act: bfloat16 [512, 32768], P(None, ('seq', 'span')), may hold values from -6 to 6
- up_weight: bfloat16 [5120, 32768], P(None, ('seq', 'span')), may hold values from -0.078125 to 0.078125
- span_counts: int32 [16], replicated, may hold values from 16 to 48, as said below
- row_ticks: int32 [512], replicated, may hold values from 0 to 47, as said below
- encoder_out: bfloat16 [8, 384, 1280], P('span'), may hold values from -6 to 6
- mlp_input: bfloat16 [8, 384, 1280], P('span'), may hold values from -6 to 6
- post_gain: float32 [1280], replicated, may hold values from 0.5 to 1.5
- post_bias: float32 [1280], replicated, may hold values from -3 to 3
- adapter_in: bfloat16 [5120, 5120], P(None, 'seq'), may hold values from -0.078125 to 0.078125
- adapter_out: bfloat16 [5120, 5120], P('seq'), may hold values from -0.078125 to 0.078125
- expand_weight: bfloat16 [1280, 5120], P(None, 'seq'), may hold values from -0.15625 to 0.15625
- expand_bias: float32 [5120], P('seq'), may hold values from -3 to 3
- contract_weight: bfloat16 [5120, 1280], P('seq'), may hold values from -0.078125 to 0.078125
Outputs:
- gate_act_grad: bfloat16 [512, 32768], P(None, ('seq', 'span'))
- up_weight_grad: bfloat16 [5120, 32768], P(None, ('seq', 'span'))
- adapter_in_grad: bfloat16 [5120, 5120], P('span', 'seq')
- adapter_out_grad: bfloat16 [5120, 5120], P(('seq', 'span'))
- expand_weight_grad: bfloat16 [1280, 5120], P('span', 'seq')
- contract_weight_grad: bfloat16 [5120, 1280], P(('seq', 'span'))
- expand_bias_grad: float32 [5120], P('seq')
- post_gain_grad: float32 [1280], replicated
- post_bias_grad: float32 [1280], replicated
- contract_bias_grad: float32 [1280], replicated
- encoder_out_grad: bfloat16 [8, 384, 1280], P('span', 'seq')
- mlp_input_grad: bfloat16 [8, 384, 1280], P('span', 'seq')
Inputs may be any that keep to these rules, and one draw needn't show every extreme that they name: span_counts sums to 512; its largest entry is exactly 48. `row_ticks`: the rows of each span are consecutive in the sequence, spans in order of their number, span k holding span_counts[k] rows; inside a span the tick rises by one from row to row.
All inputs are finite; a program needn't handle non-finite values.
Results may differ from a plain program's by a relative error of at most 0.03.
Values may be sent and summed in bfloat16 or wider, within the bound.
A program may use at most 192 MiB of HBM per device.

v0:
```python
import math
import jax
import jax.numpy as jnp
from jax import lax
from jax.sharding import PartitionSpec as P

STACK = 4
CH_DEV = 2
EPSILON = 1e-05


def gelu_value(values):
    return 0.5 * values * (1.0 + lax.erf(values * (1.0 / math.sqrt(2.0))))


def gelu_slope(values):
    cumulative = 0.5 * (1.0 + lax.erf(values * (1.0 / math.sqrt(2.0))))
    return cumulative + values * jnp.exp(-0.5 * values * values) * (1.0 / math.sqrt(2.0 * math.pi))


def locate_rows(span_counts, row_ticks, capacity):
    span_ends = jnp.cumsum(span_counts)
    positions = jnp.arange(row_ticks.shape[0], dtype=jnp.int32)
    span_of = jnp.sum((positions[:, None] >= span_ends[None, :]).astype(jnp.int32), axis=1)
    return span_of * capacity + row_ticks


def contract_last(left, right):
    return lax.dot_general(
        left, right, (((1,), (1,)), ((), ())), preferred_element_type=jnp.float32
    )


def contract_first(left, right):
    return lax.dot_general(
        left, right, (((0,), (0,)), ((), ())), preferred_element_type=jnp.float32
    )


def per_device(
    llm_input,
    hidden_grad,
    gate_act,
    up_weight,
    span_counts,
    row_ticks,
    encoder_out,
    mlp_input,
    post_gain,
    post_bias,
    adapter_in,
    adapter_out,
    expand_weight,
    expand_bias,
    contract_weight,
):
    rows_all = row_ticks.shape[0]
    up_grad = (hidden_grad.astype(jnp.float32) * gate_act.astype(jnp.float32)).astype(jnp.bfloat16)
    frames_each = encoder_out.shape[1]
    width = encoder_out.shape[2]
    slots_each = frames_each // STACK
    capacity = slots_each // CH_DEV
    owner_count = lax.axis_size("span")
    slot_of = locate_rows(span_counts, row_ticks, capacity)
    total_slots = owner_count * slots_each
    matches = jnp.arange(total_slots, dtype=jnp.int32)[:, None] == slot_of[None, :]
    filled = jnp.any(matches, axis=1)
    source = jnp.sum(jnp.where(matches, jnp.arange(rows_all, dtype=jnp.int32)[None, :], 0), axis=1)
    picked = jnp.take(up_grad, source, axis=0) * filled[:, None].astype(jnp.bfloat16)
    partial_slots = lax.psum_scatter(
        contract_last(picked, up_weight).astype(jnp.bfloat16),
        "span",
        scatter_dimension=0,
        tiled=True,
    )
    token_grad = lax.psum(partial_slots, "seq")
    piece = lax.all_gather(llm_input, ("seq", "span"), axis=0, tiled=True)
    weight_sum = contract_first(piece, up_grad)
    block = jnp.dot(piece, up_weight, preferred_element_type=jnp.float32)
    up_rows = block
    weight_sum, up_rows = (weight_sum, up_rows)
    gate_act_grad = (hidden_grad.astype(jnp.float32) * up_rows).astype(jnp.bfloat16)
    up_weight_grad = weight_sum.astype(jnp.bfloat16)
    frames = encoder_out[0].astype(jnp.float32)
    centre = frames - jnp.mean(frames, axis=1, keepdims=True)
    rstd = lax.rsqrt(jnp.mean(centre * centre, axis=1, keepdims=True) + EPSILON)
    nhat = centre * rstd
    stacked = (nhat * post_gain + post_bias).reshape(slots_each, STACK * width).astype(jnp.bfloat16)
    pre_act = jnp.dot(stacked, adapter_in, preferred_element_type=jnp.float32)
    activity = gelu_value(pre_act).astype(jnp.bfloat16)
    act_grad = contract_last(token_grad, adapter_out)
    pre_grad = (act_grad * gelu_slope(pre_act)).astype(jnp.bfloat16)
    partial_out = contract_first(activity, token_grad)
    partial_in = contract_first(stacked, pre_grad)
    adapter_in_sum, adapter_out_sum = (
        lax.psum_scatter(
            partial_in.astype(jnp.bfloat16), "span", scatter_dimension=0, tiled=True
        ).astype(jnp.float32),
        lax.psum_scatter(
            partial_out.astype(jnp.bfloat16), "span", scatter_dimension=0, tiled=True
        ).astype(jnp.float32),
    )
    stacked_part = contract_last(pre_grad, adapter_in)
    mine_frames = frames_each // lax.axis_size("seq")
    seq_index = lax.axis_index("seq")
    normed_grad = (
        lax.psum(stacked_part.astype(jnp.bfloat16), "seq")
        .astype(jnp.float32)
        .reshape(frames_each, width)
    )
    scaled = normed_grad * post_gain
    resid = rstd * (
        scaled
        - jnp.mean(scaled, axis=1, keepdims=True)
        - nhat * jnp.mean(scaled * nhat, axis=1, keepdims=True)
    )
    resid = resid.astype(jnp.bfloat16)
    gain_part = jnp.sum(normed_grad * nhat, axis=0)
    shift_part = jnp.sum(normed_grad, axis=0)
    out_bias_part = jnp.sum(resid.astype(jnp.float32), axis=0)
    resid_mine = lax.dynamic_slice_in_dim(resid, seq_index * mine_frames, mine_frames, 0)
    inputs = mlp_input[0]
    hidden_pre = jnp.dot(inputs, expand_weight, preferred_element_type=jnp.float32) + expand_bias
    hidden_act = gelu_value(hidden_pre).astype(jnp.bfloat16)
    hidden_enc_grad = contract_last(resid, contract_weight)
    hidden_pre_grad = (hidden_enc_grad * gelu_slope(hidden_pre)).astype(jnp.bfloat16)
    partial_expand = contract_first(inputs, hidden_pre_grad)
    partial_contract = contract_first(hidden_act, resid)
    expand_sum, contract_sum = (
        lax.psum_scatter(
            partial_expand.astype(jnp.bfloat16), "span", scatter_dimension=0, tiled=True
        ).astype(jnp.float32),
        lax.psum_scatter(
            partial_contract.astype(jnp.bfloat16), "span", scatter_dimension=0, tiled=True
        ).astype(jnp.float32),
    )
    in_bias_part = jnp.sum(hidden_pre_grad.astype(jnp.float32), axis=0)
    mlp_part = contract_last(hidden_pre_grad, expand_weight)
    mlp_input_grad = lax.psum_scatter(
        mlp_part.astype(jnp.bfloat16), "seq", scatter_dimension=0, tiled=True
    )
    expand_bias_grad, post_gain_grad, post_bias_grad, contract_bias_grad = lax.psum(
        (in_bias_part, gain_part, shift_part, out_bias_part), "span"
    )
    return (
        gate_act_grad,
        up_weight_grad,
        adapter_in_sum.astype(jnp.bfloat16),
        adapter_out_sum.astype(jnp.bfloat16),
        expand_sum.astype(jnp.bfloat16),
        contract_sum.astype(jnp.bfloat16),
        expand_bias_grad,
        post_gain_grad,
        post_bias_grad,
        contract_bias_grad,
        resid_mine.reshape(1, mine_frames, width),
        mlp_input_grad.reshape(1, mine_frames, width),
    )


def solution(mesh):
    return jax.shard_map(
        per_device,
        mesh=mesh,
        in_specs=(
            P(("seq", "span"), None),
            P(None, ("seq", "span")),
            P(None, ("seq", "span")),
            P(None, ("seq", "span")),
            P(),
            P(),
            P("span", None, None),
            P("span", None, None),
            P(),
            P(),
            P(None, "seq"),
            P("seq", None),
            P(None, "seq"),
            P("seq"),
            P("seq", None),
        ),
        out_specs=(
            P(None, ("seq", "span")),
            P(None, ("seq", "span")),
            P("span", "seq"),
            P(("seq", "span"), None),
            P("span", "seq"),
            P(("seq", "span"), None),
            P("seq"),
            P(),
            P(),
            P(),
            P("span", "seq", None),
            P("span", "seq", None),
        ),
        check_vma=False,
    )
```

profile of v0, /device:TPU:0, one launch (start us, length us, event | category | flops | bytes accessed | tf_op | source)
XLA Modules:
  0.0 915.3 jit_solution(14220045984964570281)
XLA Ops:
  10.4 2.9 fusion.7
  13.3 5.9 gather_fusion
  19.2 13.5 %convolution_convert_fusion.2 = bf16[768,5120]{1,0:T(8,128)(2,1)} fusion(bf16[5120,1024]{1,0:T(8,128)(2,1)} %param.18, bf16[768,1024]{1,0:T(8,128)(2,1)} %gather_fusion, pred[768]{0:T(1024)(128)(4,1)S(1)} %compare_and_fusion, bf16[768]{0:T(1024)(128)(2,1)S(1)} %convert_element_type.111), kind=kOutput, calls=%fused_computation.4 | convolution fusion | flops 8058568704 | bytes 19925248 | tf_op jit(solution)/shard_map/dot_general | solution.py:29
  42.8 4.2 add_convert_fusion
  47.0 128.9 %reduce-scatter.9.cloned.1.call-done = bf16[96,5120]{1,0:T(8,128)(2,1)} async-done(((bf16[768,5120]{1,0:T(8,128)(2,1)}), bf16[96,5120]{1,0:T(8,128)(2,1)}) %reduce-scatter.9.cloned.1.call-update) | async-done | bytes 983056 | tf_op jit(solution)/shard_map/reduce_scatter | solution.py:70
  176.1 8.0 fusion.37
  184.1 29.1 %all-reduce.4.cloned.1.call-done = bf16[96,5120]{1,0:T(8,128)(2,1)} async-done(((bf16[96,5120]{1,0:T(8,128)(2,1)}), bf16[96,5120]{1,0:T(8,128)(2,1)}) %all-reduce.4.cloned.1.call-update) | async-done | bytes 983056 | tf_op jit(solution)/shard_map/psum | solution.py:76
  213.2 9.2 %fusion.5 = bf16[96,1280]{1,0:T(8,128)(2,1)S(1)} fusion(bf16[96,5120]{1,0:T(8,128)(2,1)} %all-reduce.4.cloned.1.call-done, bf16[1280,5120]{1,0:T(8,128)(2,1)} %param.26, f32[96,1280]{1,0:T(8,128)} %fusion.37), kind=kOutput, calls=%fused_computation.23 | convolution fusion | flops 1259520000 | bytes 14827520 | tf_op jit(solution)/shard_map/dot_general | solution.py:29
  222.4 9.7 %convolution_convert_fusion.5 = bf16[96,5120]{1,0:T(8,128)(2,1)} fusion(bf16[96,1280]{1,0:T(8,128)(2,1)S(1)} %fusion.5, bf16[5120,1280]{1,0:T(8,128)(2,1)} %param.25), kind=kOutput, calls=%fused_computation.8 | convolution fusion | flops 1258782720 | bytes 14336000 | tf_op jit(solution)/shard_map/dot_general | solution.py:29
  235.5 3.9 convolution_add_fusion
  239.4 36.7 %all-reduce.6.cloned.1.call-done = bf16[384,1280]{1,0:T(8,128)(2,1)} async-done(((bf16[384,1280]{1,0:T(8,128)(2,1)}), bf16[384,1280]{1,0:T(8,128)(2,1)}) %all-reduce.6.cloned.1.call-update) | async-done | bytes 983056 | tf_op jit(solution)/shard_map/psum | solution.py:107
  280.3 3.8 convert_reduce_fusion.2
  287.5 3.4 fusion
  290.9 3.4 copy.39
  296.4 3.7 convolution_convert_fusion.3
  301.3 6.6 convolution_convert_fusion.1
  309.2 6.7 convolution_convert_fusion
  317.1 10.6 %convert_bitcast_fusion = bf16[5120,1024]{0,1:T(8,128)(2,1)} fusion(bf16[512,1024]{1,0:T(8,128)(2,1)S(1)} %copy-done.2, bf16[512,5120]{1,0:T(8,128)(2,1)} %all-gather.2.cloned.1.call-done), kind=kOutput, calls=%fused_computation.3 | convolution fusion | flops 5373952000 | bytes 16777216 | tf_op jit(solution)/shard_map/dot_general | solution.py:35
  327.7 14.5 %copy.37 = bf16[5120,1024]{1,0:T(8,128)(2,1)} copy(bf16[5120,1024]{0,1:T(8,128)(2,1)} %convert_bitcast_fusion) | data formatting | bytes 20971520
  342.2 11.0 %fusion.6 = bf16[512,1024]{1,0:T(8,128)(2,1)} fusion(bf16[512,1024]{1,0:T(8,128)(2,1)} %param.16, bf16[512,5120]{1,0:T(8,128)(2,1)} %all-gather.2.cloned.1.call-done, bf16[5120,1024]{1,0:T(8,128)(2,1)} %param.18), kind=kOutput, calls=%fused_computation.24 | convolution fusion | flops 5370281984 | bytes 17825792 | tf_op jit(solution)/shard_map/dot_general | solution.py:79
  353.2 38.6 %all-reduce = (f32[1280]{0:T(1024)}, f32[1280]{0:T(1024)}, f32[1280]{0:T(1024)}, f32[1280]{0:T(1024)}) all-reduce(f32[1280]{0:T(1024)S(1)} %get-tuple-element.70, f32[1280]{0:T(1024)S(1)} %get-tuple-element.60, f32[1280]{0:T(1024)S(1)} %get-tuple-element.63, f32[1280]{0:T(1024)S(1)} %copy-done.11), channel_id=1, replica_groups=mesh['seq'=4,'span'=8] {'span'}, use_global_device_ids=true, to_apply=%region_16.17 | all-reduce | flops 5120 | bytes 40960 | tf_op jit(solution)/shard_map/psum | solution.py:142
  393.4 77.9 %reduce-scatter.15.cloned.1.call-done = bf16[160,1280]{1,0:T(8,128)(2,1)} async-done(((bf16[1280,1280]{1,0:T(8,128)(2,1)}), bf16[160,1280]{1,0:T(8,128)(2,1)}) %reduce-scatter.15.cloned.1.call-update) | async-done | bytes 409616 | tf_op jit(solution)/shard_map/reduce_scatter | solution.py:133
  471.3 218.4 %reduce-scatter.11.cloned.1.call-done = bf16[640,1280]{1,0:T(8,128)(2,1)} async-done(((bf16[5120,1280]{1,0:T(8,128)(2,1)}), bf16[640,1280]{1,0:T(8,128)(2,1)}) %reduce-scatter.11.cloned.1.call-update) | async-done | bytes 1638416 | tf_op jit(solution)/shard_map/reduce_scatter | solution.py:96
  689.7 218.1 %reduce-scatter.13.cloned.1.call-done = bf16[160,5120]{1,0:T(8,128)(2,1)} async-done(((bf16[1280,5120]{1,0:T(8,128)(2,1)}), bf16[160,5120]{1,0:T(8,128)(2,1)}) %reduce-scatter.13.cloned.1.call-update) | async-done | bytes 1638416 | tf_op jit(solution)/shard_map/reduce_scatter | solution.py:99
  (87 shorter events, 30.8 us)
Async XLA Ops:
  8.0 227.5 %copy-start = (bf16[1280,1280]{1,0:T(8,128)(2,1)S(1)}, bf16[1280,1280]{1,0:T(8,128)(2,1)}, u32[]{:S(2)}) copy-start(bf16[1280,1280]{1,0:T(8,128)(2,1)} %param.27) | copy-start | bytes 9830404
  8.0 167.8 %reduce-scatter.9.cloned.1.call-start = ((), (), s32[]{:S(2)}) async-start(), calls=%async_computation.7 | async-start | bytes 8847360 | tf_op jit(solution)/shard_map/reduce_scatter | solution.py:70
  32.8 180.4 %all-reduce.4.cloned.1.call-start = ((), (), s32[]{:S(2)}) async-start(), calls=%async_computation.8 | async-start | bytes 1966080 | tf_op jit(solution)/shard_map/psum | solution.py:76
  41.0 1.7 copy-start.12
  41.0 1.7 copy-start.10
  175.9 100.3 %all-reduce.6.cloned.1.call-start = ((), (), s32[]{:S(2)}) async-start(), calls=%async_computation.11 | async-start | bytes 1966080 | tf_op jit(solution)/shard_map/psum | solution.py:107
  232.2 3.4 copy-start.13
  234.7 81.3 %all-gather.2.cloned.1.call-start = ((), (), s32[]{:S(2)}) async-start(), calls=%async_computation.6 | async-start | bytes 5406720 | tf_op jit(solution)/shard_map/all_gather | solution.py:77
  235.2 158.2 %reduce-scatter.17.cloned.1.call-start = ((), (), s32[]{:S(2)}) async-start(), calls=%async_computation.13 | async-start | bytes 1228800 | tf_op jit(solution)/shard_map/reduce_scatter | solution.py:139
  276.1 2.6 copy-start.3
  276.1 2.6 copy-start.7
  278.7 1.6 copy-start.14
  280.1 3.9 copy-start.8
  287.5 106.0 %reduce-scatter.19.cloned.1.call-start = ((), (), s32[]{:S(2)}) async-start(), calls=%async_computation.14 | async-start | bytes 3686400
  294.4 1.3 copy-start.9
  294.4 2.0 copy-start.15
  294.4 176.9 %reduce-scatter.15.cloned.1.call-start = ((), (), s32[]{:S(2)}) async-start(), calls=%async_computation.12 | async-start | bytes 3686400 | tf_op jit(solution)/shard_map/reduce_scatter | solution.py:133
  300.1 1.2 copy-start.4
  300.1 389.6 %reduce-scatter.11.cloned.1.call-start = ((), (), s32[]{:S(2)}) async-start(), calls=%async_computation.9 | async-start | bytes 14745600 | tf_op jit(solution)/shard_map/reduce_scatter | solution.py:96
  307.8 1.4 copy-start.6
  307.9 599.9 %reduce-scatter.13.cloned.1.call-start = ((), (), s32[]{:S(2)}) async-start(), calls=%async_computation.10 | async-start | bytes 14745600 | tf_op jit(solution)/shard_map/reduce_scatter | solution.py:99
  315.9 1.2 copy-start.2
  342.2 11.0 %copy-start.11 = (f32[1280]{0:T(1024)S(1)}, f32[1280]{0:T(1024)}, u32[]{:S(2)}) copy-start(f32[1280]{0:T(1024)} %get-tuple-element.68) | copy-start | bytes 15364
  342.2 565.6 %copy-start.1 = (bf16[1280,1280]{1,0:T(8,128)(2,1)S(1)}, bf16[1280,1280]{1,0:T(8,128)(2,1)}, u32[]{:S(2)}) copy-start(bf16[1280,1280]{1,0:T(8,128)(2,1)} %param.27) | copy-start | bytes 9830404
  (2 other events, 2.0 us)
Sparse Core Ops, SparseCore 0:
  32.9 142.9 reduce-scatter.8
  178.2 34.9 all-reduce.3
  234.8 41.3 all-reduce.5
  287.6 24.4 reduce-scatter.16
  316.1 76.0 reduce-scatter.18
  396.2 75.0 reduce-scatter.14
  475.6 214.0 reduce-scatter.10
  693.9 213.8 reduce-scatter.12
Sparse Core Ops, SparseCore 1:
  238.0 67.4 all-gather.1
where the time goes:
time: 916 us; the launch traced here: 915 us
  waiting for transfers between devices  710 us (78%)
  matrix products  92.6 us (10%)
  local copies, waits for them, and re-layouts  42 us (5%)
  blocking collectives  38.6 us (4%)
  between operations  15.8 us (2%)
  other arithmetic  15.5 us (2%)
    reduce_scatter x1, waiting for transfers between devices, per_device(): lax.psum_scatter(partial_in.astype(jnp.bfloat16), 'span', scatter_dimensi...  218 us
    reduce_scatter x1, waiting for transfers between devices, per_device(): lax.psum_scatter(partial_out.astype(jnp.bfloat16), 'span', scatter_dimens...  218 us
    reduce_scatter x1, waiting for transfers between devices, per_device(): lax.psum_scatter(contract_last(picked, up_weight).astype(jnp.bfloat16), '...  129 us
    reduce_scatter x1, waiting for transfers between devices, per_device(): lax.psum_scatter(partial_contract.astype(jnp.bfloat16), 'span', scatter_d...  77.9 us
    dot_general x5, matrix products, contract_last(): lax.dot_general(left, right, (((1,), (1,)), ((), ())), preferred_element_...  38.7 us
    psum x1, blocking collectives, per_device(): lax.psum((in_bias_part, gain_part, shift_part, out_bias_part), 'span')  38.6 us
    psum x1, waiting for transfers between devices, per_device(): lax.psum(stacked_part.astype(jnp.bfloat16), 'seq').astype(jnp.float32)  36.7 us
    dot_general x5, matrix products, contract_first(): lax.dot_general(left, right, (((0,), (0,)), ((), ())), preferred_element_...  31 us
  transfers between devices with their start and end apart: 9, of which 6 were waited for; matrix products, arithmetic and copies ran while one was open for 11% of the time, Pallas kernels for 0%

commit v1 on v0

--- a/solution.py
+++ b/solution.py
@@ -104,7 +104,7 @@
     mine_frames = frames_each // lax.axis_size("seq")
     seq_index = lax.axis_index("seq")
     normed_grad = (
-        lax.psum(stacked_part.astype(jnp.bfloat16), "seq")
+        jnp.sum(lax.all_gather(stacked_part.astype(jnp.bfloat16), "seq"), axis=0)
         .astype(jnp.float32)
         .reshape(frames_each, width)
     )

time: 916 us -> 963 us (1.051)
  waiting for transfers between devices: 710 us -> 756 us
    psum x1 -> x0, waiting for transfers between devices: 36.7 us -> none  [per_device(): lax.psum(stacked_part.astype(jnp.bfloat16), 'seq').astype(jnp.float32)]
    unnamed x10, waiting for transfers between devices: 0.65 us -> 32.7 us
    all_gather x0 -> x1, waiting for transfers between devices: none -> 28.7 us  [per_device(): lax.all_gather(stacked_part.astype(jnp.bfloat16), 'seq')]
    all_gather x1, waiting for transfers between devices: 0.03 us -> 21.5 us  [per_device(): piece = lax.all_gather(llm_input, ('seq', 'span'), axis=0, tiled=True)]
  transfers between devices with their start and end apart: 9 -> 9, of which waited for: 6 -> 8; matrix products, arithmetic and copies ran while one was open for 11% -> 11% of each run, Pallas kernels for 0% -> 0%
where the time goes in v1:
time: 963 us; the launch traced here: 962 us
  waiting for transfers between devices  756 us (79%)
  matrix products  92 us (10%)
  local copies, waits for them, and re-layouts  41.4 us (4%)
  blocking collectives  37.4 us (4%)
  other arithmetic  19.7 us (2%)
  between operations  14.1 us (1%)
    reduce_scatter x1, waiting for transfers between devices, per_device(): lax.psum_scatter(partial_in.astype(jnp.bfloat16), 'span', scatter_dimensi...  218 us
    reduce_scatter x1, waiting for transfers between devices, per_device(): lax.psum_scatter(partial_out.astype(jnp.bfloat16), 'span', scatter_dimens...  218 us
    reduce_scatter x1, waiting for transfers between devices, per_device(): lax.psum_scatter(contract_last(picked, up_weight).astype(jnp.bfloat16), '...  129 us
    reduce_scatter x1, waiting for transfers between devices, per_device(): lax.psum_scatter(partial_contract.astype(jnp.bfloat16), 'span', scatter_d...  79.1 us
    dot_general x5, matrix products, contract_last(): lax.dot_general(left, right, (((1,), (1,)), ((), ())), preferred_element_...  38.2 us
    psum x1, blocking collectives, per_device(): lax.psum((in_bias_part, gain_part, shift_part, out_bias_part), 'span')  37.4 us
    unnamed x10, waiting for transfers between devices  32.7 us
    dot_general x5, matrix products, contract_first(): lax.dot_general(left, right, (((0,), (0,)), ((), ())), preferred_element_...  31 us
  transfers between devices with their start and end apart: 9, of which 8 were waited for; matrix products, arithmetic and copies ran while one was open for 11% of the time, Pallas kernels for 0%

profile of v1, /device:TPU:0, one launch (start us, length us, event | category | flops | bytes accessed | tf_op | source)
XLA Modules:
  0.0 962.0 jit_solution(16226346290992361996)
XLA Ops:
  12.5 5.9 gather_fusion
  18.4 13.5 %convolution_convert_fusion.2 = bf16[768,5120]{1,0:T(8,128)(2,1)} fusion(bf16[5120,1024]{1,0:T(8,128)(2,1)} %param.18, bf16[768,1024]{1,0:T(8,128)(2,1)} %gather_fusion, pred[768]{0:T(1024)(128)(4,1)S(1)} %compare_and_fusion, bf16[768]{0:T(1024)(128)(2,1)S(1)} %convert_element_type.119), kind=kOutput, calls=%fused_computation.4 | convolution fusion | flops 8058568704 | bytes 19925248 | tf_op jit(solution)/shard_map/dot_general | solution.py:29
  41.9 4.2 add_convert_fusion
  46.1 128.9 %reduce-scatter.9.cloned.1.call-done = bf16[96,5120]{1,0:T(8,128)(2,1)} async-done(((bf16[768,5120]{1,0:T(8,128)(2,1)}), bf16[96,5120]{1,0:T(8,128)(2,1)}) %reduce-scatter.9.cloned.1.call-update) | async-done | bytes 983056 | tf_op jit(solution)/shard_map/reduce_scatter | solution.py:70
  175.3 8.0 fusion.28
  183.3 29.1 %all-reduce.3.cloned.1.call-done = bf16[96,5120]{1,0:T(8,128)(2,1)} async-done(((bf16[96,5120]{1,0:T(8,128)(2,1)}), bf16[96,5120]{1,0:T(8,128)(2,1)}) %all-reduce.3.cloned.1.call-update) | async-done | bytes 983056 | tf_op jit(solution)/shard_map/psum | solution.py:76
  212.4 9.2 fusion.2
  221.6 9.7 %convolution_convert_fusion.5 = bf16[96,5120]{1,0:T(8,128)(2,1)} fusion(bf16[96,1280]{1,0:T(8,128)(2,1)S(1)} %fusion.2, bf16[5120,1280]{1,0:T(8,128)(2,1)} %param.25), kind=kOutput, calls=%fused_computation.8 | convolution fusion | flops 1258782720 | bytes 14336000 | tf_op jit(solution)/shard_map/dot_general | solution.py:29
  232.2 3.9 convolution_add_fusion
  236.1 28.7 %all-gather.6.cloned.1.call-done = bf16[384,5120]{1,0:T(8,128)(2,1)} async-done(((bf16[96,5120]{1,0:T(8,128)(2,1)}), bf16[384,5120]{1,0:T(8,128)(2,1)}) %all-gather.6.cloned.1.call-update) | async-done | bytes 3932176 | tf_op jit(solution)/shard_map/all_gather | solution.py:107
  264.8 4.0 reduce_sum.109
  286.5 3.4 copy.39
  291.8 3.7 convolution_convert_fusion.3
  296.7 6.6 convolution_convert_fusion.1
  304.7 6.7 convolution_convert_fusion
  311.4 21.5 %all-gather.4.cloned.1.call-done = bf16[512,5120]{1,0:T(8,128)(2,1)} async-done(((bf16[16,5120]{1,0:T(8,128)(2,1)}), bf16[512,5120]{1,0:T(8,128)(2,1)}) %all-gather.4.cloned.1.call-update) | async-done | bytes 5242896 | tf_op jit(solution)/shard_map/all_gather | solution.py:77
  332.9 10.6 %convert_bitcast_fusion = bf16[5120,1024]{0,1:T(8,128)(2,1)} fusion(bf16[512,1024]{1,0:T(8,128)(2,1)S(1)} %copy-done.2, bf16[512,5120]{1,0:T(8,128)(2,1)} %all-gather.4.cloned.1.call-done), kind=kOutput, calls=%fused_computation.3 | convolution fusion | flops 5373952000 | bytes 16777216 | tf_op jit(solution)/shard_map/dot_general | solution.py:35
  343.5 14.4 %copy.37 = bf16[5120,1024]{1,0:T(8,128)(2,1)} copy(bf16[5120,1024]{0,1:T(8,128)(2,1)} %convert_bitcast_fusion) | data formatting | bytes 20971520
  357.9 10.9 %fusion.3 = bf16[512,1024]{1,0:T(8,128)(2,1)} fusion(bf16[512,1024]{1,0:T(8,128)(2,1)} %param.16, bf16[512,5120]{1,0:T(8,128)(2,1)} %all-gather.4.cloned.1.call-done, bf16[5120,1024]{1,0:T(8,128)(2,1)} %param.18), kind=kOutput, calls=%fused_computation.18 | convolution fusion | flops 5370281984 | bytes 17825792 | tf_op jit(solution)/shard_map/dot_general | solution.py:79
  368.9 37.4 %all-reduce = (f32[1280]{0:T(1024)}, f32[1280]{0:T(1024)}, f32[1280]{0:T(1024)}, f32[1280]{0:T(1024)}) all-reduce(f32[1280]{0:T(1024)S(1)} %get-tuple-element.70, f32[1280]{0:T(1024)S(1)} %get-tuple-element.60, f32[1280]{0:T(1024)S(1)} %get-tuple-element.63, f32[1280]{0:T(1024)S(1)} %copy-done.11), channel_id=1, replica_groups=mesh['seq'=4,'span'=8] {'span'}, use_global_device_ids=true, to_apply=%region_16.17 | all-reduce | flops 5120 | bytes 40960 | tf_op jit(solution)/shard_map/psum | solution.py:142
  407.9 32.0 %reduce-scatter.19.cloned.1.call-done = bf16[160,1280]{1,0:T(8,128)(2,1)} async-done(((bf16[1280,1280]{1,0:T(8,128)(2,1)}), bf16[160,1280]{1,0:T(8,128)(2,1)}) %reduce-scatter.19.cloned.1.call-update) | async-done | bytes 409616
  439.9 79.1 %reduce-scatter.15.cloned.1.call-done = bf16[160,1280]{1,0:T(8,128)(2,1)} async-done(((bf16[1280,1280]{1,0:T(8,128)(2,1)}), bf16[160,1280]{1,0:T(8,128)(2,1)}) %reduce-scatter.15.cloned.1.call-update) | async-done | bytes 409616 | tf_op jit(solution)/shard_map/reduce_scatter | solution.py:133
  519.0 218.4 %reduce-scatter.11.cloned.1.call-done = bf16[640,1280]{1,0:T(8,128)(2,1)} async-done(((bf16[5120,1280]{1,0:T(8,128)(2,1)}), bf16[640,1280]{1,0:T(8,128)(2,1)}) %reduce-scatter.11.cloned.1.call-update) | async-done | bytes 1638416 | tf_op jit(solution)/shard_map/reduce_scatter | solution.py:96
  737.3 218.1 %reduce-scatter.13.cloned.1.call-done = bf16[160,5120]{1,0:T(8,128)(2,1)} async-done(((bf16[1280,5120]{1,0:T(8,128)(2,1)}), bf16[160,5120]{1,0:T(8,128)(2,1)}) %reduce-scatter.13.cloned.1.call-update) | async-done | bytes 1638416 | tf_op jit(solution)/shard_map/reduce_scatter | solution.py:99
  (88 shorter events, 40.0 us)
Async XLA Ops:
  7.2 225.0 %copy-start = (bf16[1280,1280]{1,0:T(8,128)(2,1)S(1)}, bf16[1280,1280]{1,0:T(8,128)(2,1)}, u32[]{:S(2)}) copy-start(bf16[1280,1280]{1,0:T(8,128)(2,1)} %param.27) | copy-start | bytes 9830404
  7.2 167.8 %reduce-scatter.9.cloned.1.call-start = ((), (), s32[]{:S(2)}) async-start(), calls=%async_computation.7 | async-start | bytes 8847360 | tf_op jit(solution)/shard_map/reduce_scatter | solution.py:70
  31.9 180.4 %all-reduce.3.cloned.1.call-start = ((), (), s32[]{:S(2)}) async-start(), calls=%async_computation.8 | async-start | bytes 1966080 | tf_op jit(solution)/shard_map/psum | solution.py:76
  40.2 1.7 copy-start.12
  40.2 1.7 copy-start.10
  175.0 89.8 %all-gather.6.cloned.1.call-start = ((), (), s32[]{:S(2)}) async-start(), calls=%async_computation.13 | async-start | bytes 4915200 | tf_op jit(solution)/shard_map/all_gather | solution.py:107
  221.6 10.6 %copy-start.14 = (f32[1280]{0:T(1024)S(1)}, f32[1280]{0:T(1024)}, u32[]{:S(2)}) copy-start(f32[1280]{0:T(1024)} %param.28) | copy-start | bytes 15364
  231.3 101.5 %all-gather.4.cloned.1.call-start = ((), (), s32[]{:S(2)}) async-start(), calls=%async_computation.6 | async-start | bytes 5406720 | tf_op jit(solution)/shard_map/all_gather | solution.py:77
  231.9 176.0 %reduce-scatter.17.cloned.1.call-start = ((), (), s32[]{:S(2)}) async-start(), calls=%async_computation.12 | async-start | bytes 1228800 | tf_op jit(solution)/shard_map/reduce_scatter | solution.py:139
  271.5 2.8 copy-start.3
  271.5 2.8 copy-start.4
  274.3 2.0 copy-start.13
  275.6 4.0 copy-start.8
  283.1 156.8 %reduce-scatter.19.cloned.1.call-start = ((), (), s32[]{:S(2)}) async-start(), calls=%async_computation.14 | async-start | bytes 3686400
  290.0 1.2 copy-start.9
  290.0 1.9 copy-start.15
  290.0 229.0 %reduce-scatter.15.cloned.1.call-start = ((), (), s32[]{:S(2)}) async-start(), calls=%async_computation.11 | async-start | bytes 3686400 | tf_op jit(solution)/shard_map/reduce_scatter | solution.py:133
  295.5 1.2 copy-start.5
  295.5 441.8 %reduce-scatter.11.cloned.1.call-start = ((), (), s32[]{:S(2)}) async-start(), calls=%async_computation.9 | async-start | bytes 14745600 | tf_op jit(solution)/shard_map/reduce_scatter | solution.py:96
  303.3 1.4 copy-start.7
  303.3 652.1 %reduce-scatter.13.cloned.1.call-start = ((), (), s32[]{:S(2)}) async-start(), calls=%async_computation.10 | async-start | bytes 14745600 | tf_op jit(solution)/shard_map/reduce_scatter | solution.py:99
  311.3 21.6 %copy-start.2 = (bf16[512,1024]{1,0:T(8,128)(2,1)S(1)}, bf16[512,1024]{1,0:T(8,128)(2,1)}, u32[]{:S(2)}) copy-start(bf16[512,1024]{1,0:T(8,128)(2,1)} %fusion.4) | copy-start | bytes 3145732
  357.9 10.9 %copy-start.11 = (f32[1280]{0:T(1024)S(1)}, f32[1280]{0:T(1024)}, u32[]{:S(2)}) copy-start(f32[1280]{0:T(1024)} %get-tuple-element.68) | copy-start | bytes 15364
  357.9 597.5 %copy-start.1 = (bf16[1280,1280]{1,0:T(8,128)(2,1)S(1)}, bf16[1280,1280]{1,0:T(8,128)(2,1)}, u32[]{:S(2)}) copy-start(bf16[1280,1280]{1,0:T(8,128)(2,1)} %param.27) | copy-start | bytes 9830404
  (2 other events, 2.0 us)
Sparse Core Ops, SparseCore 0:
  32.1 142.8 reduce-scatter.8
  177.4 34.9 all-reduce.2
  231.5 33.3 all-gather.5
  267.5 65.3 all-gather.3
  335.9 22.8 reduce-scatter.16
  362.8 77.0 reduce-scatter.18
  444.1 74.8 reduce-scatter.14
  523.2 214.1 reduce-scatter.10
  741.6 213.8 reduce-scatter.12
